TPU v7x, 256 devices: a whole 4x4x8 slice. The times are simulated.
256 devices in a mesh: grp: 8 (over y, core), dev: 32 (over x, z).
Axes of the slice: x: 4, y: 4, z: 8, core: 2. Of those that a mesh axis runs over, the one named last changes fastest.
Arguments:
- particle_pos: float32 [2, 4194304], P(None, ('grp', 'dev')), may hold values from -1 to 1
- particle_mass: float32 [4194304], P(('grp', 'dev')), may hold values from 0.02 to 0.2
- leaf_counts: int32 [65536], P(('grp', 'dev')), may hold values from 1 to 64, 3145728 in all
Outputs:
- lens_field: float32 [4, 4194304], P(None, ('grp', 'dev'))
Inputs may be any that keep to these rules, and one draw needn't show every extreme that they name: `leaf_counts`: every leaf holds 1 to 64 live particles and some leaf exactly 64; the counts sum to 3145728.
All inputs are finite; a program needn't handle non-finite values. No bound on the sum of `leaf_counts` on one device may be relied on, other than what follows from the above.
Results may differ from a plain program's by a relative error of at most 0.0001.
Values sent between devices are 32-bit elements; how exact they have to be, the bound alone decides.
A program may use at most 192 MiB of HBM per device.

v0:
```python
import jax
import jax.numpy as jnp
from jax import lax
from jax.sharding import PartitionSpec as P

NODES = 6
PPL = 64
LSIDE = 16
SOFTEN = 0.01
PRECISE = lax.Precision.HIGHEST


def partner(block, axis, distance):
    count = lax.axis_size(axis)
    route = []
    for low in range(count):
        high = low | 1 << distance
        if high != low and high < count:
            route += [(low, high), (high, low)]
    return lax.ppermute(block, axis, route)


def node_angles():
    return (2.0 * jnp.arange(NODES, dtype=jnp.float32) + 1.0) * (jnp.pi / (2.0 * NODES))


def cheb_points():
    return jnp.cos(node_angles())


def interp_basis(coords):
    angles = node_angles()
    expand = (slice(None),) + (None,) * coords.ndim
    result = jnp.zeros((NODES,) + coords.shape, jnp.float32) + 1.0 / NODES
    lower_poly = jnp.ones_like(coords)
    upper_poly = coords
    for degree in range(1, NODES):
        at_nodes = jnp.cos(degree * angles)
        result = result + 2.0 / NODES * at_nodes[expand] * upper_poly[None]
        lower_poly, upper_poly = (upper_poly, 2.0 * coords * upper_poly - lower_poly)
    return result


def kernel_vals(delta_x, delta_y):
    inv_r2 = 1.0 / (delta_x * delta_x + delta_y * delta_y + SOFTEN)
    inv_sq = inv_r2 * inv_r2
    return (
        delta_x * inv_r2,
        delta_y * inv_r2,
        (delta_y * delta_y - delta_x * delta_x) * inv_sq,
        -2.0 * delta_x * delta_y * inv_sq,
    )


def far_offsets():
    return [
        (off_x, off_y)
        for off_x in range(-3, 4)
        for off_y in range(-3, 4)
        if max(abs(off_x), abs(off_y)) >= 2
    ]


def transfer_table(half_width, off_x, off_y):
    points = cheb_points()
    node_diff = points[:, None] - points[None, :]
    delta_x = half_width * node_diff[:, None, :, None] - 2.0 * half_width * off_x
    delta_y = half_width * node_diff[None, :, None, :] - 2.0 * half_width * off_y
    kernel_set = kernel_vals(delta_x, delta_y)
    stacked = jnp.stack([term_val for term_val in kernel_set])
    return stacked.reshape(4 * NODES * NODES, NODES * NODES)


def pair_mask(size_x, size_y, off_x, off_y):
    cells_x = jnp.arange(size_x, dtype=jnp.int32)
    cells_y = jnp.arange(size_y, dtype=jnp.int32)
    keep_x = jnp.abs((cells_x + off_x) // 2 - cells_x // 2) <= 1
    keep_y = jnp.abs((cells_y + off_y) // 2 - cells_y // 2) <= 1
    return (keep_x[:, None] & keep_y[None, :]).astype(jnp.float32)


def far_field(padded, size_x, size_y, half_width):
    result = jnp.zeros((4 * NODES * NODES, size_x * size_y), jnp.float32)
    for off_x, off_y in far_offsets():
        shifted = (
            padded[:, 3 + off_x : 3 + off_x + size_x, 3 + off_y : 3 + off_y + size_y]
            * pair_mask(size_x, size_y, off_x, off_y)[None]
        )
        result = result + jnp.dot(
            transfer_table(half_width, off_x, off_y),
            shifted.reshape(NODES * NODES, size_x * size_y),
            precision=PRECISE,
            preferred_element_type=jnp.float32,
        )
    return result.reshape(4, NODES * NODES, size_x, size_y)


def child_table():
    points = cheb_points()
    sides = jnp.arange(2, dtype=jnp.float32)
    coords = -0.5 + sides[:, None] + 0.5 * points[None, :]
    per_side = jnp.transpose(interp_basis(coords), (1, 2, 0))
    product_table = per_side[:, None, :, None, :, None] * per_side[None, :, None, :, None, :]
    return product_table.reshape(2, 2, NODES * NODES, NODES * NODES)


def upward(leaf_grid):
    node_table = child_table()
    size_x = leaf_grid.shape[1] // 2
    size_y = leaf_grid.shape[2] // 2
    result = jnp.zeros((NODES * NODES, size_x * size_y), jnp.float32)
    for side_x in (0, 1):
        for side_y in (0, 1):
            child_part = leaf_grid[:, side_x::2, side_y::2].reshape(NODES * NODES, size_x * size_y)
            result = result + jnp.dot(
                node_table[side_x, side_y].T,
                child_part,
                precision=PRECISE,
                preferred_element_type=jnp.float32,
            )
    return result.reshape(NODES * NODES, size_x, size_y)


def downward(parent_local):
    node_table = child_table()
    size_x = parent_local.shape[2]
    size_y = parent_local.shape[3]
    flat_local = jnp.transpose(parent_local, (1, 0, 2, 3)).reshape(
        NODES * NODES, 4 * size_x * size_y
    )
    row_list = []
    for side_x in (0, 1):
        col_list = []
        for side_y in (0, 1):
            child_part = jnp.dot(
                node_table[side_x, side_y],
                flat_local,
                precision=PRECISE,
                preferred_element_type=jnp.float32,
            )
            col_list.append(child_part.reshape(NODES * NODES, 4, size_x, size_y))
        row_list.append(jnp.stack(col_list, axis=-1))
    stacked = jnp.stack(row_list, axis=3).reshape(NODES * NODES, 4, 2 * size_x, 2 * size_y)
    return jnp.transpose(stacked, (1, 0, 2, 3))


def moments(grid_u, grid_v, grid_w):
    basis_u = interp_basis(grid_u) * grid_w[None]
    basis_v = interp_basis(grid_v)
    result = jnp.einsum("axyp,bxyp->abxy", basis_u, basis_v, precision=PRECISE)
    return result.reshape(NODES * NODES, grid_u.shape[0], grid_u.shape[1])


def near_row(target_u, target_v, near_rows):
    size_y = target_u.shape[0]
    blocks = []
    shift_x = []
    shift_y = []
    for off_x in (-1, 0, 1):
        for off_y in (-1, 0, 1):
            blocks.append(near_rows[:, off_x + 1, off_y + 1 : off_y + 1 + size_y, :])
            shift_x.append(jnp.full((PPL,), -off_x, jnp.float32))
            shift_y.append(jnp.full((PPL,), -off_y, jnp.float32))
    sources = jnp.concatenate(blocks, axis=2)
    delta_x = jnp.concatenate(shift_x)[None, None, :] + 0.5 * (
        target_u[:, :, None] - sources[0][:, None, :]
    )
    delta_y = jnp.concatenate(shift_y)[None, None, :] + 0.5 * (
        target_v[:, :, None] - sources[1][:, None, :]
    )
    weight = sources[2][:, None, :]
    return jnp.stack(
        [jnp.sum(weight * term_val, axis=2) for term_val in kernel_vals(delta_x, delta_y)]
    )


def evaluate_row(target_u, target_v, local_row, near_rows):
    basis_u = interp_basis(target_u)
    basis_v = interp_basis(target_v)
    coeffs = local_row.reshape(4, NODES, NODES, target_u.shape[0])
    half_sum = jnp.einsum("cabq,bqp->caqp", coeffs, basis_v, precision=PRECISE)
    far_part = jnp.sum(half_sum * basis_u[None], axis=1)
    return far_part + near_row(target_u, target_v, near_rows)


def leaves_to_grid(values, axis_pos, bit_count):
    x_bits = (bit_count + 1) // 2
    y_bits = bit_count // 2
    old_shape = values.shape
    split_vals = values.reshape(old_shape[:axis_pos] + (2,) * bit_count + old_shape[axis_pos + 1 :])
    x_dims = [axis_pos + bit_count - 1 - 2 * bit_level for bit_level in range(x_bits - 1, -1, -1)]
    y_dims = [axis_pos + bit_count - 2 - 2 * bit_level for bit_level in range(y_bits - 1, -1, -1)]
    lead_dims = list(range(axis_pos))
    tail_dims = list(range(axis_pos + bit_count, split_vals.ndim))
    permuted = jnp.transpose(split_vals, lead_dims + x_dims + y_dims + tail_dims)
    return permuted.reshape(
        old_shape[:axis_pos] + (2**x_bits, 2**y_bits) + old_shape[axis_pos + 1 :]
    )


def grid_to_leaves(values, axis_pos, bit_count):
    x_bits = (bit_count + 1) // 2
    y_bits = bit_count // 2
    old_shape = values.shape
    split_vals = values.reshape(old_shape[:axis_pos] + (2,) * bit_count + old_shape[axis_pos + 2 :])
    order_dims = []
    for bit_level in range(bit_count - 1, -1, -1):
        if bit_level % 2 == 0:
            order_dims.append(axis_pos + x_bits - 1 - bit_level // 2)
        else:
            order_dims.append(axis_pos + x_bits + y_bits - 1 - (bit_level - 1) // 2)
    lead_dims = list(range(axis_pos))
    tail_dims = list(range(axis_pos + bit_count, split_vals.ndim))
    permuted = jnp.transpose(split_vals, lead_dims + order_dims + tail_dims)
    return permuted.reshape(old_shape[:axis_pos] + (2**bit_count,) + old_shape[axis_pos + 2 :])


def morton_split(code_val, bit_count):
    coord_x = code_val * 0
    coord_y = code_val * 0
    for bit_level in range((bit_count + 1) // 2):
        coord_x = coord_x + code_val // 4**bit_level % 2 * 2**bit_level
        coord_y = coord_y + code_val // (2 * 4**bit_level) % 2 * 2**bit_level
    return (coord_x, coord_y)


def cut_moments(moment_grid, strip_kind):
    if strip_kind == 0:
        return moment_grid[:, :3, :]
    if strip_kind == 1:
        return moment_grid[:, -3:, :]
    if strip_kind == 2:
        return jnp.swapaxes(moment_grid[:, :, :3], 1, 2)
    return jnp.swapaxes(moment_grid[:, :, -3:], 1, 2)


def cut_particles(particles, strip_kind):
    if strip_kind == 0:
        return particles[:, 0]
    if strip_kind == 1:
        return particles[:, -1]
    if strip_kind == 2:
        return particles[:, :, 0]
    return particles[:, :, -1]


def corner(strip_vals, off_x, off_y, use_x):
    along_y = strip_vals[:, :, -3:] if off_y < 0 else strip_vals[:, :, :3]
    along_x = strip_vals[:, :, -3:] if off_x < 0 else strip_vals[:, :, :3]
    return jnp.where(use_x, along_y, jnp.swapaxes(along_x, 1, 2))


def dot_corner(strip_vals, off_x, off_y, use_x):
    from_x = strip_vals[:, -1] if off_y < 0 else strip_vals[:, 0]
    from_y = strip_vals[:, -1] if off_x < 0 else strip_vals[:, 0]
    return jnp.where(use_x, from_x, from_y)[:, None, None]


def swap_bit(values, code_bit, dev_bits):
    if code_bit < dev_bits:
        return partner(values, "dev", code_bit)
    return partner(values, "grp", code_bit - dev_bits)


def on_device(particle_pos, particle_mass, leaf_counts):
    grp_count = lax.axis_size("grp")
    dev_count = lax.axis_size("dev")
    block_bits = (grp_count * dev_count).bit_length() - 1
    dev_bits = dev_count.bit_length() - 1
    local_bits = 2 * (LSIDE.bit_length() - 1)
    side_par = LSIDE // 2
    blocks_x = 2 ** ((block_bits + 1) // 2)
    blocks_y = 2 ** (block_bits // 2)
    live_mask = (jnp.arange(PPL, dtype=jnp.int32)[None, :] < leaf_counts[:, None]).astype(
        jnp.float32
    )
    mass_rows = particle_mass.reshape(LSIDE * LSIDE, PPL)
    mass_sum, live_sum = lax.psum(
        (jnp.sum(mass_rows * live_mask), jnp.sum(live_mask)), ("grp", "dev")
    )
    mean_mass = mass_sum / live_sum
    weights = (mass_rows - mean_mass) * live_mask
    positions = particle_pos.reshape(2, LSIDE * LSIDE, PPL)
    grid_u = leaves_to_grid(positions[0], 0, local_bits)
    grid_v = leaves_to_grid(positions[1], 0, local_bits)
    grid_w = leaves_to_grid(weights, 0, local_bits)
    leaf_moments = moments(grid_u, grid_v, grid_w)
    parent_moments = upward(leaf_moments)
    particles = jnp.stack([grid_u, grid_v, grid_w])
    packed = jnp.stack(
        [
            jnp.concatenate(
                [
                    cut_moments(leaf_moments, strip_kind).ravel(),
                    cut_moments(parent_moments, strip_kind).ravel(),
                    cut_particles(particles, strip_kind).ravel(),
                ]
            )
            for strip_kind in range(4)
        ]
    )
    leaf_len = NODES * NODES * 3 * LSIDE
    par_len = NODES * NODES * 3 * side_par

    def unpack(vector):
        return (
            vector[:leaf_len].reshape(NODES * NODES, 3, LSIDE),
            vector[leaf_len : leaf_len + par_len].reshape(NODES * NODES, 3, side_par),
            vector[leaf_len + par_len :].reshape(3, LSIDE, PPL),
        )

    block_id = lax.axis_index("grp") * dev_count + lax.axis_index("dev")
    block_x, block_y = morton_split(block_id, block_bits)
    x_carry = jnp.stack([packed[1], packed[0]])
    for bit_level in range((block_bits + 1) // 2):
        taken = swap_bit(x_carry, 2 * bit_level, dev_bits)
        low_part = block_x % 2**bit_level
        x_carry = jnp.stack(
            [
                jnp.where(low_part == 0, taken[0], x_carry[0]),
                jnp.where(low_part == 2**bit_level - 1, taken[1], x_carry[1]),
            ]
        )
    y_carry = jnp.stack(
        [
            jnp.stack([packed[3], x_carry[0], x_carry[1]]),
            jnp.stack([packed[2], x_carry[0], x_carry[1]]),
        ]
    )
    for bit_level in range(block_bits // 2):
        taken = swap_bit(y_carry, 2 * bit_level + 1, dev_bits)
        low_part = block_y % 2**bit_level
        y_carry = jnp.stack(
            [
                jnp.where(low_part == 0, taken[0], y_carry[0]),
                jnp.where(low_part == 2**bit_level - 1, taken[1], y_carry[1]),
            ]
        )
    near_vecs = {
        (-1, 0): x_carry[0],
        (1, 0): x_carry[1],
        (0, -1): y_carry[0, 0],
        (0, 1): y_carry[1, 0],
        (-1, -1): y_carry[0, 1],
        (1, -1): y_carry[0, 2],
        (-1, 1): y_carry[1, 1],
        (1, 1): y_carry[1, 2],
    }

    def edge_vector(off_x, off_y):
        return near_vecs[off_x, off_y]

    tile_map = {(0, 0): (leaf_moments, parent_moments, particles)}
    for off_x in (-1, 0, 1):
        for off_y in (-1, 0, 1):
            if off_x == 0 and off_y == 0:
                continue
            near_x = block_x + off_x
            near_y = block_y + off_y
            inside = (
                (near_x >= 0) & (near_x < blocks_x) & (near_y >= 0) & (near_y < blocks_y)
            ).astype(jnp.float32)
            if off_y == 0:
                leaf_part, par_part, dot_part = unpack(edge_vector(off_x, off_y))
                pieces = (leaf_part, par_part, dot_part[:, None])
            elif off_x == 0:
                leaf_part, par_part, dot_part = unpack(edge_vector(off_x, off_y))
                pieces = (
                    jnp.swapaxes(leaf_part, 1, 2),
                    jnp.swapaxes(par_part, 1, 2),
                    dot_part[:, :, None],
                )
            else:
                vector = near_vecs[off_x, off_y]
                use_x = True
                leaf_part, par_part, dot_part = unpack(vector)
                pieces = (
                    corner(leaf_part, off_x, off_y, use_x),
                    corner(par_part, off_x, off_y, use_x),
                    dot_corner(dot_part, off_x, off_y, use_x),
                )
            tile_map[off_x, off_y] = tuple((piece_val * inside for piece_val in pieces))
    windows = []
    for member in range(3):
        columns = [
            jnp.concatenate([tile_map[off_x, off_y][member] for off_y in (-1, 0, 1)], axis=2)
            for off_x in (-1, 0, 1)
        ]
        windows.append(jnp.concatenate(columns, axis=1))
    leaf_window, par_window, part_window = windows
    parent_local = far_field(par_window, side_par, side_par, 1.0)
    leaf_local = far_field(leaf_window, LSIDE, LSIDE, 0.5) + downward(parent_local)

    def one_row(row_idx):
        near_rows = lax.dynamic_slice_in_dim(part_window, row_idx, 3, 1)
        target_u = lax.dynamic_index_in_dim(grid_u, row_idx, 0, keepdims=False)
        target_v = lax.dynamic_index_in_dim(grid_v, row_idx, 0, keepdims=False)
        local_row = lax.dynamic_index_in_dim(leaf_local, row_idx, 2, keepdims=False)
        return evaluate_row(target_u, target_v, local_row, near_rows)

    fields = lax.map(one_row, jnp.arange(LSIDE, dtype=jnp.int32))
    fields = jnp.transpose(fields, (1, 0, 2, 3))
    return grid_to_leaves(fields, 1, local_bits).reshape(4, LSIDE * LSIDE * PPL)


def solution(mesh):
    in_specs = (P(None, ("grp", "dev")), P(("grp", "dev")), P(("grp", "dev")))
    out_specs = P(None, ("grp", "dev"))
    return jax.shard_map(
        on_device, mesh=mesh, in_specs=in_specs, out_specs=out_specs, check_vma=False
    )
```

profile of v0, /device:TPU:1, one launch (start us, length us, event | category | flops | bytes accessed | tf_op | source)
XLA Modules:
  0.0 526.9 jit_solution(16787211099503064006)
XLA Ops:
  5.6 81.5 %all-reduce = (f32[]{:T(128)}, f32[]{:T(128)}) all-reduce(f32[]{:T(128)} %select_reduce_fusion, f32[]{:T(128)} %convert_reduce_fusion), channel_id=1, replica_groups=mesh['grp'=8,'dev'=32] {'grp','dev'}, use_global_device_ids=true, to_apply=%region_1.0 | all-reduce | flops 2 | bytes 16 | tf_op jit(solution)/shard_map/psum | solution.py:278
  88.8 2.6 convolution_bitcast_fusion.1
  98.2 12.1 %collective-permute-start = (f32[2,5664]{1,0:T(2,128)}, f32[2,5664]{1,0:T(2,128)}, u32[]{:S(2)}, u32[]{:S(2)}) collective-permute-start(f32[2,5664]{1,0:T(2,128)} %pad_maximum_fusion.90), channel_id=1, source_target_pairs={{0,1},{1,0},{2,3},{3,2},{4,5},{5,4},{6,7},{7,6},{8,9},{9,8},{10,11... | collective-permute-start | bytes 135944 | tf_op jit(solution)/shard_map/ppermute | solution.py:20
  112.8 2.4 broadcast_multiply_fusion.70
  115.2 3.5 broadcast_multiply_fusion.71
  119.5 3.1 broadcast_multiply_fusion.150
  122.7 4.1 broadcast_multiply_fusion.151
  175.8 3.3 collective-permute-start.1
  179.7 3.3 collective-permute-done.1
  186.9 3.0 collective-permute-done.2
  216.3 2.6 pad_maximum_fusion.2
  218.8 3.4 collective-permute-done.4
  223.5 3.1 collective-permute-done.5
  228.1 6.2 %collective-permute-start.6 = (f32[2,3,5664]{2,1,0:T(4,128)}, f32[2,3,5664]{2,1,0:T(4,128)}, u32[]{:S(2)}, u32[]{:S(2)}) collective-permute-start(f32[2,3,5664]{2,1,0:T(4,128)} %pad_maximum_fusion.82), channel_id=1, source_target_pairs={{0,32},{32,0},{64,96},{96,64},{128,160},{160,128},{192,224},{224,1... | collective-permute-start | bytes 407816 | tf_op jit(solution)/shard_map/ppermute | solution.py:20
  237.0 1.9 reshape.8441
  239.0 1.9 reshape.8435
  240.9 1.9 reshape.8431
  244.7 1.9 reshape.8421
  246.6 1.9 reshape.8417
  248.5 1.9 reshape.8411
  252.4 1.9 reshape.8403
  254.3 1.9 reshape.8391
  256.2 1.9 reshape.8387
  258.1 1.9 reshape.8381
  260.1 1.9 reshape.8377
  262.0 1.9 reshape.8373
  265.9 1.9 reshape.8369
  267.8 1.9 reshape.8371
  269.7 1.9 reshape.8375
  271.6 1.9 reshape.8379
  273.5 1.9 reshape.8383
  275.4 1.9 reshape.8385
  277.4 1.9 reshape.8389
  279.3 1.9 reshape.8393
  281.2 1.9 reshape.8395
  283.1 1.9 reshape.8397
  285.0 1.9 reshape.8399
  286.9 1.9 reshape.8401
  288.9 1.9 reshape.8405
  290.8 1.9 reshape.8409
  292.7 1.9 reshape.8415
  294.6 1.9 reshape.8419
  296.6 1.9 reshape.8423
  298.5 1.9 reshape.8425
  323.1 2.0 reshape.8284
  335.0 2.1 collective-permute-start.7
  338.2 4.8 collective-permute-done.7
  381.5 143.4 %while.13 = (s32[]{:T(128)}, f32[16,4,16,64]{3,1,2,0:T(4,128)S(1)}, s32[16]{0:T(128)S(1)}, f32[16,16,64]{2,1,0:T(8,128)S(1)}, f32[4,36,16,16]{1,0,3,2:T(4,128)S(...) while((s32[]{:T(128)}, f32[16,4,16,64]{3,1,2,0:T(4,128)S(1)}, ...), condition=%wide.region_10.11_spmd, body=%wide.region_4.10_spmd.sunk | while | flops 17893484 | bytes 1122444 | solution.py:401
  387.1 3.6 multiply_reduce_fusion.5
  396.0 3.6 multiply_reduce_fusion.5
  405.0 3.6 multiply_reduce_fusion.5
  413.9 3.6 multiply_reduce_fusion.5
  422.8 3.6 multiply_reduce_fusion.5
  431.8 3.6 multiply_reduce_fusion.5
  440.7 3.6 multiply_reduce_fusion.5
  449.7 3.6 multiply_reduce_fusion.5
  458.6 3.6 multiply_reduce_fusion.5
  467.6 3.6 multiply_reduce_fusion.5
  476.5 3.6 multiply_reduce_fusion.5
  485.4 3.6 multiply_reduce_fusion.5
  494.4 3.6 multiply_reduce_fusion.5
  503.3 3.6 multiply_reduce_fusion.5
  512.3 3.6 multiply_reduce_fusion.5
  521.2 3.6 multiply_reduce_fusion.5
  (1115 shorter events, 209.6 us)
Async XLA Ops:
  88.8 8.1 %copy-start.40 = (f32[2,2,2,2,2,2,2,2,64]{8,7,6,5,4,3,2,1,0:T(2,128)}, f32[2,2,2,2,2,2,2,2,64]{8,7,6,5,4,3,2,1,0:T(2,128)S(1)}, u32[]{:S(2)}) copy-start(f32[2,2,2,2,2,2,2,2,64]{8,7,6,5,4,3,2,1,0:T(2,128)S(1)} %copy.346) | copy-start | bytes 196612
  95.5 16.4 %copy-start.47 = (f32[2,2,36,36]{3,2,1,0:T(8,128)}, f32[2,2,36,36]{3,2,1,0:T(8,128)S(1)}, u32[]{:S(2)}) copy-start(f32[2,2,36,36]{3,2,1,0:T(8,128)S(1)} %broadcast_multiply_fusion.153) | copy-start | bytes 62212
  98.2 77.6 %collective-permute-start = (f32[2,5664]{1,0:T(2,128)}, f32[2,5664]{1,0:T(2,128)}, u32[]{:S(2)}, u32[]{:S(2)}) collective-permute-start(f32[2,5664]{1,0:T(2,128)} %pad_maximum_fusion.90), channel_id=1, source_target_pairs={{0,1},{1,0},{2,3},{3,2},{4,5},{5,4},{6,7},{7,6},{8,9},{9,8},{10,11... | collective-permute-start | bytes 135944 | tf_op jit(solution)/shard_map/ppermute | solution.py:20
  175.8 7.1 %collective-permute-start.1 = (f32[2,5664]{1,0:T(2,128)}, f32[2,5664]{1,0:T(2,128)}, u32[]{:S(2)}, u32[]{:S(2)}) collective-permute-start(f32[2,5664]{1,0:T(2,128)} %collective-permute-done), channel_id=1, source_target_pairs={{0,4},{4,0},{1,5},{5,1},{2,6},{6,2},{3,7},{7,3},{8,12},{12,8},{9,1... | collective-permute-start | bytes 135944 | tf_op jit(solution)/shard_map/ppermute | solution.py:20
  185.2 4.7 collective-permute-start.2
  192.1 21.0 %collective-permute-start.3 = (f32[2,5664]{1,0:T(2,128)}, f32[2,5664]{1,0:T(2,128)}, u32[]{:S(2)}, u32[]{:S(2)}) collective-permute-start(f32[2,5664]{1,0:T(2,128)} %pad_maximum_fusion.92), channel_id=1, source_target_pairs={{0,64},{64,0},{32,96},{96,32},{128,192},{192,128},{160,224},{224,1... | collective-permute-start | bytes 135944 | tf_op jit(solution)/shard_map/ppermute | solution.py:20
  214.9 7.3 %collective-permute-start.4 = (f32[2,3,5664]{2,1,0:T(4,128)S(1)}, f32[2,3,5664]{2,1,0:T(4,128)S(1)}, u32[]{:S(2)}, u32[]{:S(2)}) collective-permute-start(f32[2,3,5664]{2,1,0:T(4,128)S(1)} %pad_maximum_fusion.81), channel_id=1, source_target_pairs={{0,2},{2,0},{1,3},{3,1},{4,6},{6,4},{5,7},{7,5},{8,10},{10,8},{9,1... | collective-permute-start | bytes 407816 | tf_op jit(solution)/shard_map/ppermute | solution.py:20
  216.2 6.1 %copy-start.49 = (f32[1,6,6,6,6]{2,1,0,4,3:T(8,128)S(1)}, f32[1,6,6,6,6]{2,1,0,4,3:T(8,128)}, u32[]{:S(2)}) copy-start(f32[1,6,6,6,6]{2,1,0,4,3:T(8,128)} %get-tuple-element.528) | copy-start | bytes 15556
  216.2 6.1 %copy-start.50 = (f32[1,6,6,6,6]{2,1,0,4,3:T(8,128)S(1)}, f32[1,6,6,6,6]{2,1,0,4,3:T(8,128)}, u32[]{:S(2)}) copy-start(f32[1,6,6,6,6]{2,1,0,4,3:T(8,128)} %get-tuple-element.542) | copy-start | bytes 15556
  216.2 6.1 %copy-start.51 = (f32[1,6,6,6,6]{2,1,0,4,3:T(8,128)S(1)}, f32[1,6,6,6,6]{2,1,0,4,3:T(8,128)}, u32[]{:S(2)}) copy-start(f32[1,6,6,6,6]{2,1,0,4,3:T(8,128)} %get-tuple-element.543) | copy-start | bytes 15556
  216.2 6.1 %copy-start.52 = (f32[1,6,6,6,6]{2,1,0,4,3:T(8,128)S(1)}, f32[1,6,6,6,6]{2,1,0,4,3:T(8,128)}, u32[]{:S(2)}) copy-start(f32[1,6,6,6,6]{2,1,0,4,3:T(8,128)} %get-tuple-element.546) | copy-start | bytes 15556
  216.2 6.1 %copy-start.53 = (f32[1,6,6,6,6]{2,1,0,4,3:T(8,128)S(1)}, f32[1,6,6,6,6]{2,1,0,4,3:T(8,128)}, u32[]{:S(2)}) copy-start(f32[1,6,6,6,6]{2,1,0,4,3:T(8,128)} %get-tuple-element.673) | copy-start | bytes 15556
  216.2 6.1 %copy-start.54 = (f32[1,6,6,6,6]{2,1,0,4,3:T(8,128)S(1)}, f32[1,6,6,6,6]{2,1,0,4,3:T(8,128)}, u32[]{:S(2)}) copy-start(f32[1,6,6,6,6]{2,1,0,4,3:T(8,128)} %get-tuple-element.827) | copy-start | bytes 15556
  216.2 6.1 %copy-start.55 = (f32[1,6,6,6,6]{2,1,0,4,3:T(8,128)S(1)}, f32[1,6,6,6,6]{2,1,0,4,3:T(8,128)}, u32[]{:S(2)}) copy-start(f32[1,6,6,6,6]{2,1,0,4,3:T(8,128)} %get-tuple-element.828) | copy-start | bytes 15556
  216.2 6.1 %copy-start.56 = (f32[1,6,6,6,6]{2,1,0,4,3:T(8,128)S(1)}, f32[1,6,6,6,6]{2,1,0,4,3:T(8,128)}, u32[]{:S(2)}) copy-start(f32[1,6,6,6,6]{2,1,0,4,3:T(8,128)} %get-tuple-element.836) | copy-start | bytes 15556
  222.3 4.4 collective-permute-start.5
  228.1 105.8 %collective-permute-start.6 = (f32[2,3,5664]{2,1,0:T(4,128)}, f32[2,3,5664]{2,1,0:T(4,128)}, u32[]{:S(2)}, u32[]{:S(2)}) collective-permute-start(f32[2,3,5664]{2,1,0:T(4,128)} %pad_maximum_fusion.82), channel_id=1, source_target_pairs={{0,32},{32,0},{64,96},{96,64},{128,160},{160,128},{192,224},{224,1... | collective-permute-start | bytes 407816 | tf_op jit(solution)/shard_map/ppermute | solution.py:20
  321.4 3.7 copy-start.35
  322.3 3.7 copy-start.32
  323.1 3.7 copy-start.30
  335.0 8.0 %collective-permute-start.7 = (f32[2,3,5664]{2,1,0:T(4,128)S(1)}, f32[2,3,5664]{2,1,0:T(4,128)S(1)}, u32[]{:S(2)}, u32[]{:S(2)}) collective-permute-start(f32[2,3,5664]{2,1,0:T(4,128)S(1)} %pad_maximum_fusion.83), channel_id=1, source_target_pairs={{0,128},{128,0},{32,160},{160,32},{64,192},{192,64},{96,224},{224,... | collective-permute-start | bytes 407816 | tf_op jit(solution)/shard_map/ppermute | solution.py:20
  345.1 3.0 copy-start.184
  345.1 3.0 copy-start.256
  345.4 3.0 copy-start.175
  345.4 3.0 copy-start.243
  345.7 3.0 copy-start.163
  345.8 3.0 copy-start.242
  346.0 3.0 copy-start.173
  346.1 3.0 copy-start.241
  346.4 3.0 copy-start.172
  346.4 3.0 copy-start.240
  346.7 3.0 copy-start.171
  346.7 3.0 copy-start.239
  347.0 3.0 copy-start.170
  347.0 3.0 copy-start.238
  347.3 3.0 copy-start.169
  347.3 3.0 copy-start.237
  347.6 3.0 copy-start.156
  347.9 3.0 copy-start.167
  348.2 3.0 copy-start.153
  348.2 3.0 copy-start.255
  348.5 3.0 copy-start.166
  348.8 3.0 copy-start.152
  348.8 3.0 copy-start.236
  349.1 3.0 copy-start.165
  349.1 3.0 copy-start.235
  349.4 3.0 copy-start.151
  349.4 3.0 copy-start.234
  349.7 3.0 copy-start.164
  349.7 3.0 copy-start.233
  350.0 3.0 copy-start.150
  350.0 3.0 copy-start.232
  350.3 3.0 copy-start.162
  350.3 3.0 copy-start.231
  350.6 3.0 copy-start.161
  350.6 3.0 copy-start.230
  350.9 3.0 copy-start.183
  351.2 3.0 copy-start.160
  351.2 3.0 copy-start.229
  351.5 3.0 copy-start.149
  351.5 3.0 copy-start.228
  351.8 3.0 copy-start.159
  351.8 3.0 copy-start.227
  352.1 3.0 copy-start.148
  (205 other events, 353.6 us)
where the time goes:
time: 537 us; the launch traced here: 527 us
  local copies, waits for them, and re-layouts  160 us (30%)
  other arithmetic  145 us (27%)
  blocking collectives  81.5 us (15%)
  loops' own time  53.4 us (10%)
  matrix products  37.4 us (7%)
  starting transfers between devices  26.2 us (5%)
  waiting for transfers between devices  17.6 us (3%)
  between operations  5.99 us (1%)
    reshape x80, local copies, waits for them, and re-layouts, transfer_table(): return stacked.reshape(4 * NODES * NODES, NODES * NODES)  97.1 us
    psum x1, blocking collectives, on_device(): lax.psum((jnp.sum(mass_rows * live_mask), jnp.sum(live_mask)), ('grp', 'd...  81.5 us
    reduce_sum x16, other arithmetic, near_row(): jnp.sum(weight * term_val, axis=2)  57.3 us
    another operation x1, loops' own time, on_device(): fields = lax.map(one_row, jnp.arange(LSIDE, dtype=jnp.int32))  53.4 us
    another operation x40, other arithmetic, transfer_table(): stacked = jnp.stack([term_val for term_val in kernel_set])  48.1 us
    ppermute x8, starting transfers between devices, partner(): return lax.ppermute(block, axis, route)  26.2 us
    dot_general x80, matrix products, far_field(): jnp.dot(transfer_table(half_width, off_x, off_y), shifted.reshape(NODES *...  24.8 us
    ppermute x8, waiting for transfers between devices, partner(): return lax.ppermute(block, axis, route)  17.6 us
  transfers between devices with their start and end apart: 8, of which 5 were waited for; matrix products, arithmetic and copies ran while one was open for 36% of the time, Pallas kernels for 0%

commit v1 on v0

--- a/solution.py
+++ b/solution.py
@@ -275,9 +275,8 @@
         jnp.float32
     )
     mass_rows = particle_mass.reshape(LSIDE * LSIDE, PPL)
-    mass_sum, live_sum = lax.psum(
-        (jnp.sum(mass_rows * live_mask), jnp.sum(live_mask)), ("grp", "dev")
-    )
+    fix_slabs_up = lambda mine: lax.psum(lax.psum(mine, axis_name="grp"), axis_name="dev")
+    mass_sum, live_sum = fix_slabs_up((jnp.sum(mass_rows * live_mask), jnp.sum(live_mask)))
     mean_mass = mass_sum / live_sum
     weights = (mass_rows - mean_mass) * live_mask
     positions = particle_pos.reshape(2, LSIDE * LSIDE, PPL)

time: 537 us -> 549 us (1.022)
  starting transfers between devices: 26.2 us -> 34 us
  waiting for transfers between devices: 17.6 us -> 25 us
    ppermute x8, starting transfers between devices: 26.2 us -> 34 us  [partner(): return lax.ppermute(block, axis, route)]
    ppermute x8, waiting for transfers between devices: 17.6 us -> 25 us  [partner(): return lax.ppermute(block, axis, route)]
    psum x1 -> x2, blocking collectives: 81.5 us -> 78.3 us  [the longest x1 62.6 us: on_device(): lax.psum(lax.psum(mine, axis_name='grp'), axis_name='dev')]
  transfers between devices with their start and end apart: 8 -> 8, of which waited for: 5 -> 5; matrix products, arithmetic and copies ran while one was open for 36% -> 35% of each run, Pallas kernels for 0% -> 0%
where the time goes in v1:
time: 549 us; the launch traced here: 539 us
  local copies, waits for them, and re-layouts  160 us (29%)
  other arithmetic  145 us (26%)
  blocking collectives  78.3 us (14%)
  loops' own time  53.4 us (10%)
  matrix products  37.4 us (7%)
  starting transfers between devices  34 us (6%)
  waiting for transfers between devices  25 us (5%)
  between operations  6.16 us (1%)
    reshape x80, local copies, waits for them, and re-layouts, transfer_table(): return stacked.reshape(4 * NODES * NODES, NODES * NODES)  97.2 us
    psum x1, blocking collectives, on_device(): lax.psum(lax.psum(mine, axis_name='grp'), axis_name='dev')  62.6 us
    reduce_sum x16, other arithmetic, near_row(): jnp.sum(weight * term_val, axis=2)  57.3 us
    another operation x1, loops' own time, on_device(): fields = lax.map(one_row, jnp.arange(LSIDE, dtype=jnp.int32))  53.4 us
    another operation x40, other arithmetic, transfer_table(): stacked = jnp.stack([term_val for term_val in kernel_set])  47.9 us
    ppermute x8, starting transfers between devices, partner(): return lax.ppermute(block, axis, route)  34 us
    ppermute x8, waiting for transfers between devices, partner(): return lax.ppermute(block, axis, route)  25 us
    dot_general x80, matrix products, far_field(): jnp.dot(transfer_table(half_width, off_x, off_y), shifted.reshape(NODES *...  24.8 us
  transfers between devices with their start and end apart: 8, of which 5 were waited for; matrix products, arithmetic and copies ran while one was open for 35% of the time, Pallas kernels for 0%

profile of v1, /device:TPU:1, one launch (start us, length us, event | category | flops | bytes accessed | tf_op | source)
XLA Modules:
  0.0 538.9 jit_solution(12764998887180235161)
XLA Ops:
  5.6 15.7 %all-reduce.1 = (f32[]{:T(128)}, f32[]{:T(128)}) all-reduce(f32[]{:T(128)} %select_reduce_fusion, f32[]{:T(128)} %convert_reduce_fusion), channel_id=1, replica_groups=mesh['grp'=8,'dev'=32] {'grp'}, use_global_device_ids=true, to_apply=%region_1.0 | all-reduce | flops 2 | bytes 16 | tf_op jit(solution)/shard_map/psum | solution.py:278
  21.3 62.6 %all-reduce = (f32[]{:T(128)}, f32[]{:T(128)}) all-reduce(f32[]{:T(128)} %get-tuple-element.204, f32[]{:T(128)} %get-tuple-element.205), channel_id=1, replica_groups=mesh['grp'=8,'dev'=32] {'dev'}, use_global_device_ids=true, to_apply=%region_2.0 | all-reduce | flops 2 | bytes 16 | tf_op jit(solution)/shard_map/psum | solution.py:278
  85.8 2.6 convolution_bitcast_fusion.1
  95.2 11.5 %collective-permute-start = (f32[2,5664]{1,0:T(2,128)}, f32[2,5664]{1,0:T(2,128)}, u32[]{:S(2)}, u32[]{:S(2)}) collective-permute-start(f32[2,5664]{1,0:T(2,128)} %pad_maximum_fusion.90), channel_id=1, source_target_pairs={{0,1},{1,0},{2,3},{3,2},{4,5},{5,4},{6,7},{7,6},{8,9},{9,8},{10,11... | collective-permute-start | bytes 135944 | tf_op jit(solution)/shard_map/ppermute | solution.py:20
  109.0 2.4 broadcast_multiply_fusion.70
  111.4 3.5 broadcast_multiply_fusion.71
  115.8 3.1 broadcast_multiply_fusion.150
  118.9 4.1 broadcast_multiply_fusion.151
  172.5 6.5 %collective-permute-done.1 = f32[2,5664]{1,0:T(2,128)} collective-permute-done((f32[2,5664]{1,0:T(2,128)}, f32[2,5664]{1,0:T(2,128)}, u32[]{:S(2)}, u32[]{:S(2)}) %collective-permute-start.1) | collective-permute-done | bytes 45344 | tf_op jit(solution)/shard_map/ppermute | solution.py:20
  181.8 4.1 collective-permute-done.2
  211.2 2.6 pad_maximum_fusion.2
  213.8 4.5 collective-permute-done.4
  219.6 3.1 collective-permute-done.5
  224.1 22.1 %collective-permute-start.6 = (f32[2,3,5664]{2,1,0:T(4,128)}, f32[2,3,5664]{2,1,0:T(4,128)}, u32[]{:S(2)}, u32[]{:S(2)}) collective-permute-start(f32[2,3,5664]{2,1,0:T(4,128)} %pad_maximum_fusion.82), channel_id=1, source_target_pairs={{0,32},{32,0},{64,96},{96,64},{128,160},{160,128},{192,224},{224,1... | collective-permute-start | bytes 407816 | tf_op jit(solution)/shard_map/ppermute | solution.py:20
  247.1 1.9 reshape.8445
  250.9 1.9 reshape.8435
  252.8 1.9 reshape.8431
  254.8 1.9 reshape.8427
  256.7 1.9 reshape.8421
  258.6 1.9 reshape.8417
  260.5 1.9 reshape.8411
  262.4 1.9 reshape.8407
  264.4 1.9 reshape.8403
  268.2 1.9 reshape.8387
  270.1 1.9 reshape.8381
  272.0 1.9 reshape.8377
  274.0 1.9 reshape.8373
  275.9 1.9 reshape.8365
  277.8 1.9 reshape.8369
  279.7 1.9 reshape.8371
  281.7 1.9 reshape.8375
  283.6 1.9 reshape.8379
  285.5 1.9 reshape.8383
  287.4 1.9 reshape.8385
  289.3 1.9 reshape.8389
  291.3 1.9 reshape.8393
  293.2 1.9 reshape.8395
  295.1 1.9 reshape.8397
  297.0 1.9 reshape.8399
  299.0 1.9 reshape.8401
  300.9 1.9 reshape.8405
  302.8 1.9 reshape.8409
  304.7 1.9 reshape.8415
  306.6 1.9 reshape.8419
  310.5 1.9 reshape.8425
  335.1 2.0 reshape.8284
  348.4 6.6 %collective-permute-done.7 = f32[2,3,5664]{2,1,0:T(4,128)S(1)} collective-permute-done((f32[2,3,5664]{2,1,0:T(4,128)S(1)}, f32[2,3,5664]{2,1,0:T(4,128)S(1)}, u32[]{:S(2)}, u32[]{:S(2)}) %collective-permute-start.7) | collective-permute-done | bytes 135968 | tf_op jit(solution)/shard_map/ppermute | solution.py:20
  393.5 143.4 %while.13 = (s32[]{:T(128)}, f32[16,4,16,64]{3,1,2,0:T(4,128)S(1)}, s32[16]{0:T(128)S(1)}, f32[16,16,64]{2,1,0:T(8,128)S(1)}, f32[4,36,16,16]{1,0,3,2:T(4,128)S(...) while((s32[]{:T(128)}, f32[16,4,16,64]{3,1,2,0:T(4,128)S(1)}, ...), condition=%wide.region_12.13_spmd, body=%wide.region_6.12_spmd.sunk | while | flops 17893484 | bytes 1122444 | solution.py:400
  399.1 3.6 multiply_reduce_fusion.5
  408.0 3.6 multiply_reduce_fusion.5
  417.0 3.6 multiply_reduce_fusion.5
  425.9 3.6 multiply_reduce_fusion.5
  434.9 3.6 multiply_reduce_fusion.5
  443.8 3.6 multiply_reduce_fusion.5
  452.7 3.6 multiply_reduce_fusion.5
  461.7 3.6 multiply_reduce_fusion.5
  470.6 3.6 multiply_reduce_fusion.5
  479.6 3.6 multiply_reduce_fusion.5
  488.5 3.6 multiply_reduce_fusion.5
  497.5 3.6 multiply_reduce_fusion.5
  506.4 3.6 multiply_reduce_fusion.5
  515.3 3.6 multiply_reduce_fusion.5
  524.3 3.6 multiply_reduce_fusion.5
  533.2 3.6 multiply_reduce_fusion.5
  (1116 shorter events, 205.5 us)
Async XLA Ops:
  85.8 8.1 %copy-start.40 = (f32[2,2,2,2,2,2,2,2,64]{8,7,6,5,4,3,2,1,0:T(2,128)}, f32[2,2,2,2,2,2,2,2,64]{8,7,6,5,4,3,2,1,0:T(2,128)S(1)}, u32[]{:S(2)}) copy-start(f32[2,2,2,2,2,2,2,2,64]{8,7,6,5,4,3,2,1,0:T(2,128)S(1)} %copy.346) | copy-start | bytes 196612
  92.4 15.8 %copy-start.47 = (f32[2,2,36,36]{3,2,1,0:T(8,128)}, f32[2,2,36,36]{3,2,1,0:T(8,128)S(1)}, u32[]{:S(2)}) copy-start(f32[2,2,36,36]{3,2,1,0:T(8,128)S(1)} %broadcast_multiply_fusion.153) | copy-start | bytes 62212
  95.2 76.7 %collective-permute-start = (f32[2,5664]{1,0:T(2,128)}, f32[2,5664]{1,0:T(2,128)}, u32[]{:S(2)}, u32[]{:S(2)}) collective-permute-start(f32[2,5664]{1,0:T(2,128)} %pad_maximum_fusion.90), channel_id=1, source_target_pairs={{0,1},{1,0},{2,3},{3,2},{4,5},{5,4},{6,7},{7,6},{8,9},{9,8},{10,11... | collective-permute-start | bytes 135944 | tf_op jit(solution)/shard_map/ppermute | solution.py:20
  171.9 7.1 %collective-permute-start.1 = (f32[2,5664]{1,0:T(2,128)}, f32[2,5664]{1,0:T(2,128)}, u32[]{:S(2)}, u32[]{:S(2)}) collective-permute-start(f32[2,5664]{1,0:T(2,128)} %collective-permute-done), channel_id=1, source_target_pairs={{0,4},{4,0},{1,5},{5,1},{2,6},{6,2},{3,7},{7,3},{8,12},{12,8},{9,1... | collective-permute-start | bytes 135944 | tf_op jit(solution)/shard_map/ppermute | solution.py:20
  181.2 4.7 collective-permute-start.2
  188.2 20.9 %collective-permute-start.3 = (f32[2,5664]{1,0:T(2,128)}, f32[2,5664]{1,0:T(2,128)}, u32[]{:S(2)}, u32[]{:S(2)}) collective-permute-start(f32[2,5664]{1,0:T(2,128)} %pad_maximum_fusion.92), channel_id=1, source_target_pairs={{0,64},{64,0},{32,96},{96,32},{128,192},{192,128},{160,224},{224,1... | collective-permute-start | bytes 135944 | tf_op jit(solution)/shard_map/ppermute | solution.py:20
  211.0 7.3 %collective-permute-start.4 = (f32[2,3,5664]{2,1,0:T(4,128)S(1)}, f32[2,3,5664]{2,1,0:T(4,128)S(1)}, u32[]{:S(2)}, u32[]{:S(2)}) collective-permute-start(f32[2,3,5664]{2,1,0:T(4,128)S(1)} %pad_maximum_fusion.81), channel_id=1, source_target_pairs={{0,2},{2,0},{1,3},{3,1},{4,6},{6,4},{5,7},{7,5},{8,10},{10,8},{9,1... | collective-permute-start | bytes 407816 | tf_op jit(solution)/shard_map/ppermute | solution.py:20
  211.1 7.2 %copy-start.49 = (f32[1,6,6,6,6]{2,1,0,4,3:T(8,128)S(1)}, f32[1,6,6,6,6]{2,1,0,4,3:T(8,128)}, u32[]{:S(2)}) copy-start(f32[1,6,6,6,6]{2,1,0,4,3:T(8,128)} %get-tuple-element.530) | copy-start | bytes 15556
  211.1 7.2 %copy-start.50 = (f32[1,6,6,6,6]{2,1,0,4,3:T(8,128)S(1)}, f32[1,6,6,6,6]{2,1,0,4,3:T(8,128)}, u32[]{:S(2)}) copy-start(f32[1,6,6,6,6]{2,1,0,4,3:T(8,128)} %get-tuple-element.544) | copy-start | bytes 15556
  211.1 7.2 %copy-start.51 = (f32[1,6,6,6,6]{2,1,0,4,3:T(8,128)S(1)}, f32[1,6,6,6,6]{2,1,0,4,3:T(8,128)}, u32[]{:S(2)}) copy-start(f32[1,6,6,6,6]{2,1,0,4,3:T(8,128)} %get-tuple-element.545) | copy-start | bytes 15556
  211.1 7.2 %copy-start.52 = (f32[1,6,6,6,6]{2,1,0,4,3:T(8,128)S(1)}, f32[1,6,6,6,6]{2,1,0,4,3:T(8,128)}, u32[]{:S(2)}) copy-start(f32[1,6,6,6,6]{2,1,0,4,3:T(8,128)} %get-tuple-element.548) | copy-start | bytes 15556
  211.1 7.2 %copy-start.53 = (f32[1,6,6,6,6]{2,1,0,4,3:T(8,128)S(1)}, f32[1,6,6,6,6]{2,1,0,4,3:T(8,128)}, u32[]{:S(2)}) copy-start(f32[1,6,6,6,6]{2,1,0,4,3:T(8,128)} %get-tuple-element.675) | copy-start | bytes 15556
  211.1 7.2 %copy-start.54 = (f32[1,6,6,6,6]{2,1,0,4,3:T(8,128)S(1)}, f32[1,6,6,6,6]{2,1,0,4,3:T(8,128)}, u32[]{:S(2)}) copy-start(f32[1,6,6,6,6]{2,1,0,4,3:T(8,128)} %get-tuple-element.829) | copy-start | bytes 15556
  211.2 7.2 %copy-start.55 = (f32[1,6,6,6,6]{2,1,0,4,3:T(8,128)S(1)}, f32[1,6,6,6,6]{2,1,0,4,3:T(8,128)}, u32[]{:S(2)}) copy-start(f32[1,6,6,6,6]{2,1,0,4,3:T(8,128)} %get-tuple-element.830) | copy-start | bytes 15556
  211.2 7.2 %copy-start.56 = (f32[1,6,6,6,6]{2,1,0,4,3:T(8,128)S(1)}, f32[1,6,6,6,6]{2,1,0,4,3:T(8,128)}, u32[]{:S(2)}) copy-start(f32[1,6,6,6,6]{2,1,0,4,3:T(8,128)} %get-tuple-element.838) | copy-start | bytes 15556
  218.3 4.4 collective-permute-start.5
  224.1 121.8 %collective-permute-start.6 = (f32[2,3,5664]{2,1,0:T(4,128)}, f32[2,3,5664]{2,1,0:T(4,128)}, u32[]{:S(2)}, u32[]{:S(2)}) collective-permute-start(f32[2,3,5664]{2,1,0:T(4,128)} %pad_maximum_fusion.82), channel_id=1, source_target_pairs={{0,32},{32,0},{64,96},{96,64},{128,160},{160,128},{192,224},{224,1... | collective-permute-start | bytes 407816 | tf_op jit(solution)/shard_map/ppermute | solution.py:20
  333.4 3.7 copy-start.35
  334.3 3.7 copy-start.32
  335.1 3.7 copy-start.30
  347.0 8.0 %collective-permute-start.7 = (f32[2,3,5664]{2,1,0:T(4,128)S(1)}, f32[2,3,5664]{2,1,0:T(4,128)S(1)}, u32[]{:S(2)}, u32[]{:S(2)}) collective-permute-start(f32[2,3,5664]{2,1,0:T(4,128)S(1)} %pad_maximum_fusion.83), channel_id=1, source_target_pairs={{0,128},{128,0},{32,160},{160,32},{64,192},{192,64},{96,224},{224,... | collective-permute-start | bytes 407816 | tf_op jit(solution)/shard_map/ppermute | solution.py:20
  357.1 3.0 copy-start.184
  357.1 3.0 copy-start.256
  357.4 3.0 copy-start.175
  357.5 3.0 copy-start.243
  357.8 3.0 copy-start.163
  357.8 3.0 copy-start.242
  358.1 3.0 copy-start.173
  358.1 3.0 copy-start.241
  358.4 3.0 copy-start.172
  358.4 3.0 copy-start.240
  358.7 3.0 copy-start.171
  358.7 3.0 copy-start.239
  359.0 3.0 copy-start.170
  359.0 3.0 copy-start.238
  359.3 3.0 copy-start.169
  359.3 3.0 copy-start.237
  359.6 3.0 copy-start.156
  359.9 3.0 copy-start.167
  360.2 3.0 copy-start.153
  360.2 3.0 copy-start.255
  360.5 3.0 copy-start.166
  360.8 3.0 copy-start.152
  360.8 3.0 copy-start.236
  361.1 3.0 copy-start.165
  361.1 3.0 copy-start.235
  361.4 3.0 copy-start.151
  361.4 3.0 copy-start.234
  361.7 3.0 copy-start.164
  361.7 3.0 copy-start.233
  362.0 3.0 copy-start.150
  362.0 3.0 copy-start.232
  362.3 3.0 copy-start.162
  362.3 3.0 copy-start.231
  362.6 3.0 copy-start.161
  362.6 3.0 copy-start.230
  362.9 3.0 copy-start.183
  363.2 3.0 copy-start.160
  363.2 3.0 copy-start.229
  363.5 3.0 copy-start.149
  363.5 3.0 copy-start.228
  363.8 3.0 copy-start.159
  363.8 3.0 copy-start.227
  364.1 3.0 copy-start.148
  (205 other events, 351.3 us)
